TPU v7x, 256 devices: a whole 4x4x8 slice. The times are simulated.
256 devices in a mesh: slide: 16 (over y, x), row: 4 (over z_hi, core), col: 4 (over z_lo).
Axes of the slice: x: 4, y: 4, z: 8 (z_hi: 2, z_lo: 4; z = z_hi * 4 + z_lo), core: 2. Of those that a mesh axis runs over, the one named last changes fastest.
Arguments:
- features: bfloat16 [16, 256, 512, 256], P('slide', 'row', 'col'), may hold values from -6 to 6
- out_grad: bfloat16 [16, 256, 512, 256], P('slide', 'row', 'col'), may hold values from -6 to 6
- depth_weight: bfloat16 [9, 256], replicated, may hold values from -2 to 2
- point_weight: bfloat16 [256, 256], P(('slide', 'row', 'col')), may hold values from -0.375 to 0.375
Outputs:
- feature_grad: bfloat16 [16, 256, 512, 256], P('slide', 'row', 'col')
- point_grad: float32 [256, 256], P(('slide', 'row', 'col'))
- depth_grad: float32 [9, 256], replicated
All inputs are finite; a program needn't handle non-finite values.
Results may differ from a plain program's by a relative error of at most 0.007.
Values may be sent and summed in bfloat16 or wider, within the bound.
No kernel may reach another device: no remote copies, remote signals or barrier semaphores. Data moves between devices by JAX's collectives and lax.ppermute only.
A program may use at most 128 MiB of HBM per device.

v0:
```python
import math
import jax
import jax.numpy as jnp
from jax import lax
from jax.sharding import PartitionSpec as P


def padded(block, sides, width):
    for axis, dim in sides:
        count = lax.axis_size(axis)
        forward = [(i, i + 1) for i in range(count - 1)]
        backward = [(target, source) for source, target in forward]
        low = lax.ppermute(
            lax.slice_in_dim(block, block.shape[dim] - width, None, axis=dim), axis, forward
        )
        high = lax.ppermute(lax.slice_in_dim(block, 0, width, axis=dim), axis, backward)
        block = jnp.concatenate([low, block, high], axis=dim)
    return block


def back_project(grad_flat, point_weight):
    return lax.dot_general(
        grad_flat,
        lax.all_gather(point_weight, ("slide", "row", "col"), axis=0, tiled=True),
        (((1,), (1,)), ((), ())),
        preferred_element_type=jnp.float32,
    ).astype(jnp.bfloat16)


def on_device(features, out_grad, depth_weight, point_weight):
    rows = features.shape[1]
    cols = features.shape[2]
    chans = features.shape[3]
    total = lax.axis_size("slide") * lax.axis_size("row") * lax.axis_size("col") * rows * cols
    scale = 1.0 / math.sqrt(total)
    grad_flat = out_grad[0].reshape(rows * cols, chans)
    feat_pad = padded(features, (("row", 1), ("col", 2)), 2)[0]
    mid_grad = back_project(grad_flat, point_weight).reshape(rows, cols, chans)
    grad_pad = padded(mid_grad[None], (("row", 1), ("col", 2)), 2)[0]
    taps = depth_weight.astype(jnp.float32)
    mid = jnp.zeros((rows, cols, chans), jnp.float32)
    back = jnp.zeros((rows, cols, chans), jnp.float32)
    mid_f = mid_grad.astype(jnp.float32)
    tap_terms = []
    for a in range(3):
        for b in range(3):
            window = feat_pad[2 * a : 2 * a + rows, 2 * b : 2 * b + cols].astype(jnp.float32)
            mid = mid + taps[a * 3 + b] * window
            back = back + taps[a * 3 + b] * grad_pad[
                4 - 2 * a : 4 - 2 * a + rows, 4 - 2 * b : 4 - 2 * b + cols
            ].astype(jnp.float32)
            tap_terms.append(jnp.sum(window * mid_f, axis=(0, 1)))
    mid_flat = mid.astype(jnp.bfloat16).reshape(rows * cols, chans)
    owned = lax.psum_scatter(
        lax.dot_general(
            mid_flat, grad_flat, (((0,), (0,)), ((), ())), preferred_element_type=jnp.float32
        ),
        ("slide", "row", "col"),
        scatter_dimension=0,
        tiled=True,
    )
    depth_grad = lax.psum(jnp.stack(tap_terms), ("slide", "row", "col")) * scale
    feature_grad = back.astype(jnp.bfloat16)[None]
    return (feature_grad, owned * scale, depth_grad)


def solution(mesh):
    placed = (
        P("slide", "row", "col", None),
        P("slide", "row", "col", None),
        P(),
        P(("slide", "row", "col"), None),
    )
    return jax.shard_map(
        on_device,
        mesh=mesh,
        in_specs=placed,
        out_specs=(P("slide", "row", "col", None), P(("slide", "row", "col"), None), P()),
        check_vma=False,
    )
```

profile of v0, /device:TPU:2, one launch (start us, length us, event | category | flops | bytes accessed | tf_op | source)
XLA Modules:
  0.0 971.7 jit_solution(7291026716896225350)
XLA Ops:
  7.2 0.0 copy-start.2
  7.2 0.0 all-reduce.3.cloned.1.call-start
  7.2 1.0 fusion.22
  8.2 0.0 copy-start.3
  8.2 1.7 collective-permute-start.4
  10.0 1.3 collective-permute-start.5
  11.3 0.0 collective-permute-done.4
  11.3 2.5 constant_dynamic-update-slice_fusion.1
  13.8 6.4 collective-permute-done.5
  20.2 0.0 copy-start.1
  20.2 2.1 copy-done.1
  22.3 0.1 fusion.21
  22.4 2.9 collective-permute-start.6
  25.4 1.3 collective-permute-start.7
  26.7 0.0 copy-done.2
  26.7 0.0 copy-done.3
  26.7 585.9 %all-gather = bf16[256,1,256]{2,1,0:T(2,128)(2,1)S(1)} all-gather(bf16[1,1,256]{2,1,0:T(2,128)(2,1)S(1)} %bitcast.71), channel_id=1, replica_groups=mesh['slide'=16,'row'=4,'col'=4] {'slide','row','col'}, dimensions={0}, use_global_device_ids=true | all-gather | bytes 131584 | tf_op jit(solution)/shard_map/all_gather | solution.py:24
  612.6 0.0 collective-permute-done.6
  612.6 0.0 collective-permute-done.7
  612.6 7.2 maximum_bitcast_fusion.1
  619.8 22.3 %fusion.17 = (f32[256]{0:T(256)S(1)}, f32[256]{0:T(256)S(1)}, f32[256]{0:T(256)S(1)}, f32[256]{0:T(256)S(1)}, f32[256]{0:T(256)S(1)}, /*index=5*/f32[256]{0:T(25...) fusion(bf16[68,132,256]{2,1,0:T(8,128)(2,1)} %maximum_bitcast_fusion.1, ...), kind=kOutput, calls=%fused_computation.36 | convolution fusion | flops 1134556928 | bytes 46277632 | tf_op jit(solution)/shard_map/dot_general | solution.py:22
  642.1 0.0 copy-start
  642.1 22.8 %fusion.8 = bf16[64,128,256]{2,1,0:T(8,128)(2,1)S(1)} fusion(f32[256]{0:T(256)S(1)} %bitcast.69, f32[256]{0:T(256)S(1)} %bitcast.67, f32[256]{0:T(256)S(1)} %bitcast.65, f32[256]{0:T(256)S(1)} %bitcast.63, f32[256]{0:T(256)S(1)} %bitcast.61, f32[256]{0:T(256)S(1)} %bitcast.59, f32[256]{0:T(256)S(1)} %bitcast.57, f32[256]{0:T(256)S(1)} %bitcast.55, ...), kind=kLoop, calls=%fused_computation.27 | loop fusion | flops 56623104 | bytes 41952256 | tf_op jit(solution)/shard_map/convert_element_type | solution.py:53
  664.9 0.0 copy-done
  665.0 2.0 fusion.25
  666.9 0.0 all-reduce.3.cloned.1.call-update
  667.0 111.4 %psum.7 = f32[9,256]{1,0:T(8,128)S(1)} all-reduce(f32[9,256]{1,0:T(8,128)S(1)} %stack.39), channel_id=1, replica_groups=mesh['slide'=16,'row'=4,'col'=4] {'slide','row','col'}, use_global_device_ids=true, to_apply=%region_10.0 | all-reduce | flops 2304 | bytes 18432 | tf_op jit(solution)/shard_map/psum | solution.py:62
  778.4 1.0 fusion.23
  779.4 1.7 collective-permute-start
  781.2 1.3 collective-permute-start.1
  782.5 0.6 broadcast_multiply_fusion
  783.1 0.0 collective-permute-done
  783.1 2.5 collective-permute-done.1
  785.6 1.1 pad_maximum_fusion.2
  786.7 4.0 collective-permute-start.2
  790.7 1.3 collective-permute-start.3
  792.0 156.4 %all-reduce.3.cloned.1.call-done = f32[256,256]{1,0:T(8,128)} async-done(((f32[256,256]{1,0:T(8,128)}), f32[256,256]{1,0:T(8,128)}) %all-reduce.3.cloned.1.call-update) | async-done | bytes 262160
  948.4 1.3 dynamic-slice_multiply_fusion
  949.7 0.0 collective-permute-done.2
  949.7 0.0 collective-permute-done.3
  949.7 4.2 maximum_bitcast_fusion
  953.9 10.9 %fusion.18 = bf16[1,64,128,256]{3,2,1,0:T(8,128)(2,1)} fusion(bf16[68,132,256]{2,1,0:T(8,128)(2,1)S(1)} %maximum_bitcast_fusion, f32[256]{0:T(256)S(1)} %bitcast.70, f32[256]{0:T(256)S(1)} %bitcast.68, f32[256]{0:T(256)S(1)} %bitcast.66, f32[256]{0:T(256)S(1)} %bitcast.64, f32[256]{0:T(256)S(1)} %bitcast.62, f32[256]{0:T(256)S(1)} %bitcast.60, ...), kind=kLoop, calls=%fused_computation.40 | loop fusion | flops 56623104 | bytes 41952256 | tf_op jit(solution)/shard_map/broadcast_in_dim | solution.py:63
  (4 shorter events, 0.1 us)
Async XLA Ops:
  7.2 19.5 %copy-start.2 = (bf16[9,256]{1,0:T(8,128)(2,1)S(1)}, bf16[9,256]{1,0:T(8,128)(2,1)}, u32[]{:S(2)}) copy-start(bf16[9,256]{1,0:T(8,128)(2,1)} %param.6) | copy-start | bytes 13828
  7.2 941.2 %all-reduce.3.cloned.1.call-start = ((), (), s32[]{:S(2)}) async-start(), calls=%async_computation | async-start | bytes 524288
  8.2 18.5 %copy-start.3 = (bf16[1,256]{1,0:T(2,128)(2,1)S(1)}, bf16[1,256]{1,0:T(2,128)(2,1)}, u32[]{:S(2)}) copy-start(bf16[1,256]{1,0:T(2,128)(2,1)} %param.7) | copy-start | bytes 1540
  8.2 3.1 collective-permute-start.4
  10.0 10.2 %collective-permute-start.5 = (bf16[1,2,128,256]{3,2,1,0:T(8,128)(2,1)S(1)}, bf16[1,2,128,256]{3,2,1,0:T(8,128)(2,1)S(1)}, u32[]{:S(2)}, u32[]{:S(2)}) collective-permute-start(bf16[1,2,128,256]{3,2,1,0:T(8,128)(2,1)S(1)} %get-tuple-element.16), channel_id=1, source_target_pairs={{4,0},{8,4},{12,8},{5,1},{9,5},{13,9},{6,2},{10,6},{14,10},{7,3},{... | collective-permute-start | bytes 393224 | tf_op jit(solution)/shard_map/ppermute | solution.py:16
  20.2 2.1 copy-start.1
  22.4 590.2 %collective-permute-start.6 = (bf16[1,68,2,256]{3,2,1,0:T(2,128)(2,1)S(1)}, bf16[1,68,2,256]{3,2,1,0:T(2,128)(2,1)S(1)}, u32[]{:S(2)}, u32[]{:S(2)}) collective-permute-start(bf16[1,68,2,256]{3,2,1,0:T(2,128)(2,1)S(1)} %get-tuple-element.12), channel_id=1, source_target_pairs={{0,1},{1,2},{2,3},{4,5},{5,6},{6,7},{8,9},{9,10},{10,11},{12,13},{... | collective-permute-start | bytes 208904 | tf_op jit(solution)/shard_map/ppermute | solution.py:13
  25.4 587.2 %collective-permute-start.7 = (bf16[1,68,2,256]{3,2,1,0:T(2,128)(2,1)S(1)}, bf16[1,68,2,256]{3,2,1,0:T(2,128)(2,1)S(1)}, u32[]{:S(2)}, u32[]{:S(2)}) collective-permute-start(bf16[1,68,2,256]{3,2,1,0:T(2,128)(2,1)S(1)} %get-tuple-element.13), channel_id=1, source_target_pairs={{1,0},{2,1},{3,2},{5,4},{6,5},{7,6},{9,8},{10,9},{11,10},{13,12},{... | collective-permute-start | bytes 208904 | tf_op jit(solution)/shard_map/ppermute | solution.py:16
  642.1 22.8 %copy-start = (bf16[1,64,128,256]{3,2,1,0:T(8,128)(2,1)S(1)}, bf16[1,64,128,256]{3,2,1,0:T(8,128)(2,1)}, u32[]{:S(2)}) copy-start(bf16[1,64,128,256]{3,2,1,0:T(8,128)(2,1)} %param.5) | copy-start | bytes 12582916
  779.4 3.7 collective-permute-start
  781.2 4.4 collective-permute-start.1
  786.7 162.9 %collective-permute-start.2 = (bf16[1,68,2,256]{3,2,1,0:T(2,128)(2,1)S(1)}, bf16[1,68,2,256]{3,2,1,0:T(2,128)(2,1)S(1)}, u32[]{:S(2)}, u32[]{:S(2)}) collective-permute-start(bf16[1,68,2,256]{3,2,1,0:T(2,128)(2,1)S(1)} %get-tuple-element.14), channel_id=1, source_target_pairs={{0,1},{1,2},{2,3},{4,5},{5,6},{6,7},{8,9},{9,10},{10,11},{12,13},{... | collective-permute-start | bytes 208904 | tf_op jit(solution)/shard_map/ppermute | solution.py:13
  790.7 158.9 %collective-permute-start.3 = (bf16[1,68,2,256]{3,2,1,0:T(2,128)(2,1)S(1)}, bf16[1,68,2,256]{3,2,1,0:T(2,128)(2,1)S(1)}, u32[]{:S(2)}, u32[]{:S(2)}) collective-permute-start(bf16[1,68,2,256]{3,2,1,0:T(2,128)(2,1)S(1)} %get-tuple-element.15), channel_id=1, source_target_pairs={{1,0},{2,1},{3,2},{5,4},{6,5},{7,6},{9,8},{10,9},{11,10},{13,12},{... | collective-permute-start | bytes 208904 | tf_op jit(solution)/shard_map/ppermute | solution.py:16
Sparse Core Ops, SparseCore 0:
  667.1 281.2 all-reduce.2
where the time goes:
time: 972 us
  blocking collectives  697 us (72%)
  waiting for transfers between devices  165 us (17%)
  other arithmetic  48.2 us (5%)
  matrix products  24.3 us (2%)
  starting transfers between devices  15.6 us (2%)
  between operations  14.2 us (1%)
    all_gather x1, blocking collectives, back_project(): lax.all_gather(point_weight, ('slide', 'row', 'col'), axis=0, tiled=True)  586 us
    unnamed x2, waiting for transfers between devices  156 us
    psum x1, blocking collectives, on_device(): depth_grad = lax.psum(jnp.stack(tap_terms), ('slide', 'row', 'col')) * scale  111 us
    convert_element_type x1, other arithmetic, on_device(): mid_flat = mid.astype(jnp.bfloat16).reshape(rows * cols, chans)  22.8 us
    dot_general x1, matrix products, back_project(): lax.dot_general(grad_flat, lax.all_gather(point_weight, ('slide', 'row',...  22.3 us
  transfers between devices with their start and end apart: 9, of which 3 were waited for; matrix products, arithmetic and copies ran while one was open for 1% of the time, Pallas kernels for 0%

commit v1 on v0

--- a/solution.py
+++ b/solution.py
@@ -21,7 +21,15 @@
 def back_project(grad_flat, point_weight):
     return lax.dot_general(
         grad_flat,
-        lax.all_gather(point_weight, ("slide", "row", "col"), axis=0, tiled=True),
+        jnp.concatenate(
+            lax.all_to_all(
+                jnp.stack([point_weight] * lax.axis_size(("slide", "row", "col"))),
+                ("slide", "row", "col"),
+                0,
+                0,
+            ),
+            axis=0,
+        ),
         (((1,), (1,)), ((), ())),
         preferred_element_type=jnp.float32,
     ).astype(jnp.bfloat16)

time: 972 us -> 340 us (0.35)
  blocking collectives: 697 us -> 82.1 us
  waiting for transfers between devices: 165 us -> 145 us
  starting transfers between devices: 15.6 us -> 31.8 us
  other arithmetic: 48.2 us -> 34.5 us
    all_gather x1 -> x0, blocking collectives: 586 us -> none  [back_project(): lax.all_gather(point_weight, ('slide', 'row', 'col'), axis=0, tiled=True)]
    psum x1, blocking collectives: 111 us -> 82.1 us  [on_device(): depth_grad = lax.psum(jnp.stack(tap_terms), ('slide', 'row', 'col')) * scale]
    unnamed x2, waiting for transfers between devices: 156 us -> 137 us
    all_to_all x0 -> x1, starting transfers between devices: none -> 16.5 us  [back_project(): lax.all_to_all(jnp.stack([point_weight] * lax.axis_size(('slide', 'row',...]
    convert_element_type x1, other arithmetic: 22.8 us -> 9.92 us  [on_device(): mid_flat = mid.astype(jnp.bfloat16).reshape(rows * cols, chans)]
  transfers between devices with their start and end apart: 9 -> 10, of which waited for: 3 -> 4; matrix products, arithmetic and copies ran while one was open for 1% -> 14% of each run, Pallas kernels for 0% -> 0%
where the time goes in v1:
time: 340 us
  waiting for transfers between devices  145 us (43%)
  blocking collectives  82.1 us (24%)
  other arithmetic  34.5 us (10%)
  starting transfers between devices  31.8 us (9%)
  matrix products  24.2 us (7%)
  between operations  14.3 us (4%)
  local copies, waits for them, and re-layouts  8.06 us (2%)
    unnamed x2, waiting for transfers between devices  137 us
    psum x1, blocking collectives, on_device(): depth_grad = lax.psum(jnp.stack(tap_terms), ('slide', 'row', 'col')) * scale  82.1 us
    dot_general x1, matrix products, back_project(): lax.dot_general(grad_flat, jnp.concatenate(lax.all_to_all(jnp.stack([poin...  22.2 us
    all_to_all x1, starting transfers between devices, back_project(): lax.all_to_all(jnp.stack([point_weight] * lax.axis_size(('slide', 'row',...  16.5 us
    broadcast_in_dim x1, other arithmetic, on_device(): feature_grad = back.astype(jnp.bfloat16)[None]  10.9 us
    convert_element_type x1, other arithmetic, on_device(): mid_flat = mid.astype(jnp.bfloat16).reshape(rows * cols, chans)  9.92 us
    ppermute x4, starting transfers between devices, padded(): lax.ppermute(lax.slice_in_dim(block, block.shape[dim] - width, None, axis...  9.86 us
    ppermute x4, waiting for transfers between devices, padded(): lax.ppermute(lax.slice_in_dim(block, 0, width, axis=dim), axis, backward)  7.1 us
  transfers between devices with their start and end apart: 10, of which 4 were waited for; matrix products, arithmetic and copies ran while one was open for 14% of the time, Pallas kernels for 0%

profile of v1, /device:TPU:2, one launch (start us, length us, event | category | flops | bytes accessed | tf_op | source)
XLA Modules:
  0.0 339.6 jit_solution(11864813117959371998)
XLA Ops:
  7.2 1.0 fusion.22
  8.2 1.7 collective-permute-start.4
  9.9 0.7 reduce
  10.6 0.1 stack.22
  10.8 0.5 broadcast.4
  11.3 1.4 reduce.1
  12.7 0.7 reshape.31
  13.4 0.0 copy-start.3
  13.4 16.5 %all-to-all-start = ((bf16[256,2,128]{2,1,0:T(2,128)(2,1)}), bf16[256,2,128]{2,1,0:T(2,128)(2,1)S(1)}, u32[]{:S(2)}, u32[]{:S(2)}) async-start(bf16[256,2,128]{2,1,0:T(2,128)(2,1)} %reshape.31), calls=%async_computation | async-start | bytes 262144 | tf_op jit(solution)/shard_map/all_to_all | solution.py:25
  29.9 0.0 all-reduce.3.cloned.1.call-start
  29.9 1.3 collective-permute-start.5
  31.2 0.0 collective-permute-done.4
  31.3 2.5 constant_dynamic-update-slice_fusion.1
  33.7 0.0 collective-permute-done.5
  33.8 0.0 copy-start.2
  33.8 2.0 copy-done.2
  35.8 0.1 fusion.21
  35.9 3.5 %collective-permute-start.6 = (bf16[1,68,2,256]{3,2,1,0:T(2,128)(2,1)S(1)}, bf16[1,68,2,256]{3,2,1,0:T(2,128)(2,1)S(1)}, u32[]{:S(2)}, u32[]{:S(2)}) collective-permute-start(bf16[1,68,2,256]{3,2,1,0:T(2,128)(2,1)S(1)} %get-tuple-element.12), channel_id=1, source_target_pairs={{0,1},{1,2},{2,3},{4,5},{5,6},{6,7},{8,9},{9,10},{10,11},{12,13},{... | collective-permute-start | bytes 208904 | tf_op jit(solution)/shard_map/ppermute | solution.py:13
  39.4 1.5 collective-permute-start.7
  40.9 0.0 copy-done.3
  40.9 1.1 collective-permute-done.6
  42.0 3.6 %collective-permute-done.7 = bf16[1,68,2,256]{3,2,1,0:T(2,128)(2,1)S(1)} collective-permute-done((bf16[1,68,2,256]{3,2,1,0:T(2,128)(2,1)S(1)}, bf16[1,68,2,256]{3,2,1,0:T(2,128)(2,1)S(1)}, u32[]{:S(2)}, u32[]{:S(2)}) %collective-permute-start.7) | collective-permute-done | bytes 69664 | tf_op jit(solution)/shard_map/ppermute | solution.py:16
  45.6 4.3 %maximum_bitcast_fusion.1 = bf16[68,132,256]{2,1,0:T(8,128)(2,1)S(1)} fusion(bf16[1,68,2,256]{3,2,1,0:T(2,128)(2,1)S(1)} %collective-permute-done.7, bf16[1,68,128,256]{3,2,1,0:T(8,128)(2,1)} %copy-done.2, bf16[1,68,2,256]{3,2,1,0:T(2,128)(2,1)S(1)} %collective-permute-done.6), kind=kLoop, calls=%fused_computation.39 | loop fusion | flops 13787136 | bytes 9191424 | tf_op jit(solution)/shard_map/squeeze | solution.py:45
  49.9 0.0 copy-start
  49.9 0.0 copy-start.1
  49.9 9.9 %fusion.8 = bf16[64,128,256]{2,1,0:T(8,128)(2,1)S(1)} fusion(f32[256]{0:T(256)S(1)} %bitcast.68, f32[256]{0:T(256)S(1)} %bitcast.66, f32[256]{0:T(256)S(1)} %bitcast.64, f32[256]{0:T(256)S(1)} %bitcast.62, f32[256]{0:T(256)S(1)} %bitcast.60, f32[256]{0:T(256)S(1)} %bitcast.58, f32[256]{0:T(256)S(1)} %bitcast.56, f32[256]{0:T(256)S(1)} %bitcast.54, ...), kind=kLoop, calls=%fused_computation.27 | loop fusion | flops 56623104 | bytes 41952256 | tf_op jit(solution)/shard_map/convert_element_type | solution.py:61
  59.9 0.0 copy-done
  59.9 0.0 copy-done.1
  59.9 2.0 fusion.25
  61.9 0.0 all-reduce.3.cloned.1.call-update
  61.9 0.0 all-to-all-done
  62.0 22.2 %fusion.17 = (f32[256]{0:T(256)S(1)}, f32[256]{0:T(256)S(1)}, f32[256]{0:T(256)S(1)}, f32[256]{0:T(256)S(1)}, f32[256]{0:T(256)S(1)}, /*index=5*/f32[256]{0:T(25...) fusion(bf16[68,132,256]{2,1,0:T(8,128)(2,1)} %copy-done, ...), kind=kOutput, calls=%fused_computation.36 | convolution fusion | flops 1134556928 | bytes 46277632 | tf_op jit(solution)/shard_map/dot_general | solution.py:22
  84.2 82.1 %psum.7 = f32[9,256]{1,0:T(8,128)S(1)} all-reduce(f32[9,256]{1,0:T(8,128)S(1)} %stack.32), channel_id=1, replica_groups=mesh['slide'=16,'row'=4,'col'=4] {'slide','row','col'}, use_global_device_ids=true, to_apply=%region_10.0 | all-reduce | flops 2304 | bytes 18432 | tf_op jit(solution)/shard_map/psum | solution.py:70
  166.3 1.0 fusion.23
  167.3 1.5 collective-permute-start
  168.8 1.3 collective-permute-start.1
  170.1 0.6 broadcast_multiply_fusion
  170.7 0.0 collective-permute-done
  170.7 3.5 %collective-permute-done.1 = bf16[1,2,128,256]{3,2,1,0:T(8,128)(2,1)S(1)} collective-permute-done((bf16[1,2,128,256]{3,2,1,0:T(8,128)(2,1)S(1)}, bf16[1,2,128,256]{3,2,1,0:T(8,128)(2,1)S(1)}, u32[]{:S(2)}, u32[]{:S(2)}) %collective-permute-start.1) | collective-permute-done | bytes 131104 | tf_op jit(solution)/shard_map/ppermute | solution.py:16
  174.2 1.1 pad_maximum_fusion.2
  175.3 3.1 collective-permute-start.2
  178.5 1.3 collective-permute-start.3
  179.8 136.6 %all-reduce.3.cloned.1.call-done = f32[256,256]{1,0:T(8,128)} async-done(((f32[256,256]{1,0:T(8,128)}), f32[256,256]{1,0:T(8,128)}) %all-reduce.3.cloned.1.call-update) | async-done | bytes 262160
  316.3 1.3 dynamic-slice_multiply_fusion
  317.6 0.0 collective-permute-done.2
  317.6 0.0 collective-permute-done.3
  317.6 4.2 %maximum_bitcast_fusion = bf16[68,132,256]{2,1,0:T(8,128)(2,1)S(1)} fusion(bf16[1,68,2,256]{3,2,1,0:T(2,128)(2,1)S(1)} %collective-permute-done.3, bf16[1,2,128,256]{3,2,1,0:T(8,128)(2,1)S(1)} %collective-permute-done.1, bf16[1,64,128,256]{3,2,1,0:T(8,128)(2,1)} %bitcast.49, bf16[1,2,128,256]{3,2,1,0:T(8,128)(2,1)S(1)} %collective-permute-done, ...), kind=kLoop, calls=%fused_computation.38 | loop fusion | flops 22978560 | bytes 9191424 | tf_op jit(solution)/shard_map/squeeze | solution.py:47
  321.8 10.9 %fusion.18 = bf16[1,64,128,256]{3,2,1,0:T(8,128)(2,1)} fusion(bf16[68,132,256]{2,1,0:T(8,128)(2,1)S(1)} %maximum_bitcast_fusion, f32[256]{0:T(256)S(1)} %bitcast.69, f32[256]{0:T(256)S(1)} %bitcast.67, f32[256]{0:T(256)S(1)} %bitcast.65, f32[256]{0:T(256)S(1)} %bitcast.63, f32[256]{0:T(256)S(1)} %bitcast.61, f32[256]{0:T(256)S(1)} %bitcast.59, ...), kind=kLoop, calls=%fused_computation.40 | loop fusion | flops 56623104 | bytes 41952256 | tf_op jit(solution)/shard_map/broadcast_in_dim | solution.py:71
  (5 shorter events, 0.1 us)
Async XLA Ops:
  8.2 23.1 %collective-permute-start.4 = (bf16[1,2,128,256]{3,2,1,0:T(8,128)(2,1)S(1)}, bf16[1,2,128,256]{3,2,1,0:T(8,128)(2,1)S(1)}, u32[]{:S(2)}, u32[]{:S(2)}) collective-permute-start(bf16[1,2,128,256]{3,2,1,0:T(8,128)(2,1)S(1)} %get-tuple-element.17), channel_id=1, source_target_pairs={{0,4},{4,8},{8,12},{1,5},{5,9},{9,13},{2,6},{6,10},{10,14},{3,7},{... | collective-permute-start | bytes 393224 | tf_op jit(solution)/shard_map/ppermute | solution.py:13
  13.4 27.5 %copy-start.3 = (bf16[9,256]{1,0:T(8,128)(2,1)S(1)}, bf16[9,256]{1,0:T(8,128)(2,1)}, u32[]{:S(2)}) copy-start(bf16[9,256]{1,0:T(8,128)(2,1)} %param.6) | copy-start | bytes 13828
  13.4 48.6 %all-to-all-start = ((bf16[256,2,128]{2,1,0:T(2,128)(2,1)}), bf16[256,2,128]{2,1,0:T(2,128)(2,1)S(1)}, u32[]{:S(2)}, u32[]{:S(2)}) async-start(bf16[256,2,128]{2,1,0:T(2,128)(2,1)} %reshape.31), calls=%async_computation | async-start | bytes 262144 | tf_op jit(solution)/shard_map/all_to_all | solution.py:25
  29.9 286.4 %all-reduce.3.cloned.1.call-start = ((), (), s32[]{:S(2)}) async-start(), calls=%async_computation.1 | async-start | bytes 524288
  29.9 3.8 %collective-permute-start.5 = (bf16[1,2,128,256]{3,2,1,0:T(8,128)(2,1)S(1)}, bf16[1,2,128,256]{3,2,1,0:T(8,128)(2,1)S(1)}, u32[]{:S(2)}, u32[]{:S(2)}) collective-permute-start(bf16[1,2,128,256]{3,2,1,0:T(8,128)(2,1)S(1)} %get-tuple-element.16), channel_id=1, source_target_pairs={{4,0},{8,4},{12,8},{5,1},{9,5},{13,9},{6,2},{10,6},{14,10},{7,3},{... | collective-permute-start | bytes 393224 | tf_op jit(solution)/shard_map/ppermute | solution.py:16
  33.8 2.0 copy-start.2
  35.9 6.1 %collective-permute-start.6 = (bf16[1,68,2,256]{3,2,1,0:T(2,128)(2,1)S(1)}, bf16[1,68,2,256]{3,2,1,0:T(2,128)(2,1)S(1)}, u32[]{:S(2)}, u32[]{:S(2)}) collective-permute-start(bf16[1,68,2,256]{3,2,1,0:T(2,128)(2,1)S(1)} %get-tuple-element.12), channel_id=1, source_target_pairs={{0,1},{1,2},{2,3},{4,5},{5,6},{6,7},{8,9},{9,10},{10,11},{12,13},{... | collective-permute-start | bytes 208904 | tf_op jit(solution)/shard_map/ppermute | solution.py:13
  39.4 6.2 %collective-permute-start.7 = (bf16[1,68,2,256]{3,2,1,0:T(2,128)(2,1)S(1)}, bf16[1,68,2,256]{3,2,1,0:T(2,128)(2,1)S(1)}, u32[]{:S(2)}, u32[]{:S(2)}) collective-permute-start(bf16[1,68,2,256]{3,2,1,0:T(2,128)(2,1)S(1)} %get-tuple-element.13), channel_id=1, source_target_pairs={{1,0},{2,1},{3,2},{5,4},{6,5},{7,6},{9,8},{10,9},{11,10},{13,12},{... | collective-permute-start | bytes 208904 | tf_op jit(solution)/shard_map/ppermute | solution.py:16
  49.9 10.0 %copy-start = (bf16[68,132,256]{2,1,0:T(8,128)(2,1)}, bf16[68,132,256]{2,1,0:T(8,128)(2,1)S(1)}, u32[]{:S(2)}) copy-start(bf16[68,132,256]{2,1,0:T(8,128)(2,1)S(1)} %maximum_bitcast_fusion.1) | copy-start | bytes 13787140
  49.9 10.0 %copy-start.1 = (bf16[1,64,128,256]{3,2,1,0:T(8,128)(2,1)S(1)}, bf16[1,64,128,256]{3,2,1,0:T(8,128)(2,1)}, u32[]{:S(2)}) copy-start(bf16[1,64,128,256]{3,2,1,0:T(8,128)(2,1)} %param.5) | copy-start | bytes 12582916
  167.3 3.4 %collective-permute-start = (bf16[1,2,128,256]{3,2,1,0:T(8,128)(2,1)S(1)}, bf16[1,2,128,256]{3,2,1,0:T(8,128)(2,1)S(1)}, u32[]{:S(2)}, u32[]{:S(2)}) collective-permute-start(bf16[1,2,128,256]{3,2,1,0:T(8,128)(2,1)S(1)} %get-tuple-element.18), channel_id=1, source_target_pairs={{0,4},{4,8},{8,12},{1,5},{5,9},{9,13},{2,6},{6,10},{10,14},{3,7},{... | collective-permute-start | bytes 393224 | tf_op jit(solution)/shard_map/ppermute | solution.py:13
  168.8 5.4 %collective-permute-start.1 = (bf16[1,2,128,256]{3,2,1,0:T(8,128)(2,1)S(1)}, bf16[1,2,128,256]{3,2,1,0:T(8,128)(2,1)S(1)}, u32[]{:S(2)}, u32[]{:S(2)}) collective-permute-start(bf16[1,2,128,256]{3,2,1,0:T(8,128)(2,1)S(1)} %get-tuple-element.19), channel_id=1, source_target_pairs={{4,0},{8,4},{12,8},{5,1},{9,5},{13,9},{6,2},{10,6},{14,10},{7,3},{... | collective-permute-start | bytes 393224 | tf_op jit(solution)/shard_map/ppermute | solution.py:16
  175.3 142.2 %collective-permute-start.2 = (bf16[1,68,2,256]{3,2,1,0:T(2,128)(2,1)S(1)}, bf16[1,68,2,256]{3,2,1,0:T(2,128)(2,1)S(1)}, u32[]{:S(2)}, u32[]{:S(2)}) collective-permute-start(bf16[1,68,2,256]{3,2,1,0:T(2,128)(2,1)S(1)} %get-tuple-element.14), channel_id=1, source_target_pairs={{0,1},{1,2},{2,3},{4,5},{5,6},{6,7},{8,9},{9,10},{10,11},{12,13},{... | collective-permute-start | bytes 208904 | tf_op jit(solution)/shard_map/ppermute | solution.py:13
  178.5 139.1 %collective-permute-start.3 = (bf16[1,68,2,256]{3,2,1,0:T(2,128)(2,1)S(1)}, bf16[1,68,2,256]{3,2,1,0:T(2,128)(2,1)S(1)}, u32[]{:S(2)}, u32[]{:S(2)}) collective-permute-start(bf16[1,68,2,256]{3,2,1,0:T(2,128)(2,1)S(1)} %get-tuple-element.15), channel_id=1, source_target_pairs={{1,0},{2,1},{3,2},{5,4},{6,5},{7,6},{9,8},{10,9},{11,10},{13,12},{... | collective-permute-start | bytes 208904 | tf_op jit(solution)/shard_map/ppermute | solution.py:16
Sparse Core Ops, SparseCore 0:
  62.1 254.2 all-reduce.2
